TPU v7x, 256 devices: a whole 4x4x8 slice. The times are simulated.
256 devices in a mesh: ctx: 16 (over x, y_hi, core), grp: 16 (over y_lo, z).
Axes of the slice: x: 4, y: 4 (y_hi: 2, y_lo: 2; y = y_hi * 2 + y_lo), z: 8, core: 2. Of those that a mesh axis runs over, the one named last changes fastest.
Arguments:
- tokens: bfloat16 [65536, 2560], P(('ctx', 'grp')), may hold values from -6 to 6
- norm_gain: bfloat16 [2560], replicated, may hold values from 0.5 to 1.5
- w_query: bfloat16 [2560, 2560], P('grp'), may hold values from -0.125 to 0.125
- w_key: bfloat16 [2560, 512], P('grp'), may hold values from -0.125 to 0.125
- w_value: bfloat16 [2560, 512], P('grp'), may hold values from -0.125 to 0.125
- b_query: bfloat16 [2560], replicated, may hold values from -3 to 3
- b_key: bfloat16 [512], replicated, may hold values from -3 to 3
- b_value: bfloat16 [512], replicated, may hold values from -3 to 3
- cache_keys: bfloat16 [2048, 512], P('ctx'), may hold values from -140 to 140
- cache_values: bfloat16 [2048, 512], P('ctx'), may hold values from -6 to 6
- block_lists: int32 [20, 512, 4], P(None, ('ctx', 'grp')), may hold values from -1 to 15, as said below
- start_position: int32 [1], replicated, may hold values from 0 to 983040
Outputs:
- context: float32 [65536, 2560], P(('ctx', 'grp'))
- keys_new: float32 [65536, 512], P(('ctx', 'grp'))
- values_new: float32 [65536, 512], P(('ctx', 'grp'))
Inputs may be any that keep to these rules, and one draw needn't show every extreme that they name: `block_lists`: each list names distinct blocks of 128 prefix positions, named blocks first and -1 in the empty slots after them; every list names at least one block, some list names 4 and some only one.
All inputs are finite; a program needn't handle non-finite values.
Results may differ from a plain program's by a relative error of at most 0.034.
Values may be sent and summed in bfloat16 or wider, within the bound.
A program may use at most 128 MiB of HBM per device.

v0:
```python
import jax
import jax.numpy as jnp
import numpy as np
from jax import lax
from jax.sharding import PartitionSpec as P

HD = 128
GROUP = 5
QBLK = 128
norm_eps = 1e-06
rope_base = 10000000.0


def angle_tables(head_dim):
    half_dim = head_dim // 2
    frequency = rope_base ** (-2.0 * np.arange(half_dim) / head_dim)
    return np.stack(
        [np.mod(frequency * 32.0**digit_level, 2.0 * np.pi) for digit_level in range(4)]
    )


def rotate(values, positions):
    head_dim = values.shape[-1]
    half_dim = head_dim // 2
    tables = jnp.asarray(angle_tables(head_dim), jnp.float32)
    angles = jnp.zeros((positions.shape[0], half_dim), jnp.float32)
    remaining = positions
    for digit_level in range(4):
        digit_value = (remaining % 32).astype(jnp.float32)
        angles = angles + digit_value[:, None] * tables[digit_level][None, :]
        remaining = remaining // 32
    cosine = jnp.cos(angles)[:, None, :]
    sine_part = jnp.sin(angles)[:, None, :]
    lower_half = values[..., :half_dim]
    upper_half = values[..., half_dim:]
    return jnp.concatenate(
        [
            lower_half * cosine - upper_half * sine_part,
            upper_half * cosine + lower_half * sine_part,
        ],
        axis=-1,
    )


def on_device(
    tokens,
    norm_gain,
    w_query,
    w_key,
    w_value,
    b_query,
    b_key,
    b_value,
    cache_keys,
    cache_values,
    block_lists,
    start_position,
):
    row_count = tokens.shape[0]
    query_width = w_query.shape[1]
    kv_width = w_key.shape[1]
    heads_kv = kv_width // HD
    block_count = row_count // QBLK
    widened = tokens.astype(jnp.float32)
    normed = (
        widened
        * lax.rsqrt(jnp.mean(widened * widened, axis=-1, keepdims=True) + norm_eps)
        * norm_gain.astype(jnp.float32)
    ).astype(jnp.bfloat16)
    panels = (
        lax.all_gather(w_query, "grp", axis=0, tiled=True),
        lax.all_gather(w_key, "grp", axis=0, tiled=True),
        lax.all_gather(w_value, "grp", axis=0, tiled=True),
    )
    query_lin, key_lin, value_lin = tuple(
        (jnp.dot(normed, panel, preferred_element_type=jnp.float32) for panel in panels)
    )
    row_start = (lax.axis_index("ctx") * lax.axis_size("grp") + lax.axis_index("grp")) * row_count
    positions = start_position[0] + row_start + jnp.arange(row_count, dtype=jnp.int32)
    query = rotate(
        (query_lin + b_query.astype(jnp.float32)).reshape(row_count, heads_kv * GROUP, HD),
        positions,
    )
    keys_new = rotate(
        (key_lin + b_key.astype(jnp.float32)).reshape(row_count, heads_kv, HD), positions
    ).reshape(row_count, kv_width)
    values_new = value_lin + b_value.astype(jnp.float32)
    score_scale = HD ** (-0.5)
    query_heads = query.reshape(row_count, heads_kv, GROUP, HD)
    query_blocks = query.reshape(block_count, QBLK, heads_kv, GROUP, HD)
    key_blocks = keys_new.reshape(block_count, QBLK, heads_kv, HD)
    value_blocks = values_new.reshape(block_count, QBLK, heads_kv, HD)
    near_scores = jnp.einsum("bqkgd,bskd->kgbqs", query_blocks, key_blocks) * score_scale
    causal = lax.broadcasted_iota(jnp.int32, (QBLK, QBLK), 0) >= lax.broadcasted_iota(
        jnp.int32, (QBLK, QBLK), 1
    )
    near_scores = jnp.where(causal, near_scores, -jnp.inf)
    near_max = jnp.max(near_scores, axis=-1)
    near_exp = jnp.exp(near_scores - near_max[..., None])
    near_total = jnp.sum(near_exp, axis=-1)
    near_weighted = jnp.einsum("kgbqs,bskd->kgbqd", near_exp, value_blocks)
    initial_state = (
        near_max.reshape(heads_kv, GROUP, row_count),
        near_total.reshape(heads_kv, GROUP, row_count),
        near_weighted.reshape(heads_kv, GROUP, row_count, HD),
    )
    piece_keys = lax.all_gather(cache_keys, "ctx", axis=0, tiled=True)
    piece_values = lax.all_gather(cache_values, "ctx", axis=0, tiled=True)
    key_count = piece_keys.shape[0]

    def one_key_block(block_step, state_inner):
        old_max, old_total, old_weighted = state_inner
        block_keys = (
            lax.dynamic_slice_in_dim(piece_keys, block_step * QBLK, QBLK, 0)
            .reshape(QBLK, heads_kv, HD)
            .astype(jnp.float32)
        )
        block_values = (
            lax.dynamic_slice_in_dim(piece_values, block_step * QBLK, QBLK, 0)
            .reshape(QBLK, heads_kv, HD)
            .astype(jnp.float32)
        )
        attention_affinity = jnp.einsum("rkgd,pkd->kgrp", query_heads, block_keys) * score_scale
        listed = jnp.any(block_lists == block_step, axis=2).reshape(
            heads_kv, GROUP, block_count, 1, 1
        )
        attention_affinity = jnp.where(
            listed, attention_affinity.reshape(heads_kv, GROUP, block_count, QBLK, QBLK), -jnp.inf
        ).reshape(heads_kv, GROUP, row_count, QBLK)
        new_max = jnp.maximum(old_max, jnp.max(attention_affinity, axis=-1))
        factor = jnp.exp(old_max - new_max)
        weights = jnp.exp(attention_affinity - new_max[..., None])
        new_total = old_total * factor + jnp.sum(weights, axis=-1)
        new_weighted = old_weighted * factor[..., None] + jnp.einsum(
            "kgrp,pkd->kgrd", weights, block_values
        )
        return (new_max, new_total, new_weighted)

    final_max, row_total, weighted = lax.fori_loop(
        0, key_count // QBLK, one_key_block, initial_state
    )
    context = jnp.transpose(weighted / row_total[..., None], (2, 0, 1, 3)).reshape(
        row_count, query_width
    )
    return (context, keys_new, values_new)


def solution(mesh):
    in_specs = (
        P(("ctx", "grp"), None),
        P(),
        P("grp", None),
        P("grp", None),
        P("grp", None),
        P(),
        P(),
        P(),
        P("ctx", None),
        P("ctx", None),
        P(None, ("ctx", "grp"), None),
        P(),
    )
    out_specs = (P(("ctx", "grp"), None), P(("ctx", "grp"), None), P(("ctx", "grp"), None))
    return jax.shard_map(
        on_device, mesh=mesh, in_specs=in_specs, out_specs=out_specs, check_vma=False
    )
```

profile of v0, /device:TPU:1, one launch (start us, length us, event | category | flops | bytes accessed | tf_op | source)
XLA Modules:
  0.0 523.7 jit_solution(8601297681478014044)
XLA Ops:
  9.5 1.7 copy.59
  11.3 1.7 copy.60
  15.4 62.1 %all-gather.6.cloned.1.call-done = bf16[2560,512]{1,0:T(8,128)(2,1)} async-done(((bf16[160,512]{1,0:T(8,128)(2,1)}), bf16[2560,512]{1,0:T(8,128)(2,1)}) %all-gather.6.cloned.1.call-update) | async-done | bytes 2621456 | tf_op jit(solution)/shard_map/all_gather | solution.py:72
  77.5 2.6 convolution_add_fusion.2
  81.2 68.9 %all-gather.10.cloned.1.call-done = bf16[2560,512]{1,0:T(8,128)(2,1)} async-done(((bf16[160,512]{1,0:T(8,128)(2,1)}), bf16[2560,512]{1,0:T(8,128)(2,1)}) %all-gather.10.cloned.1.call-update) | async-done | bytes 2621456 | tf_op jit(solution)/shard_map/all_gather | solution.py:73
  150.2 2.6 convolution_add_fusion.1
  153.8 153.8 %all-gather.8.cloned.1.call-done = bf16[2560,2560]{1,0:T(8,128)(2,1)} async-done(((bf16[160,2560]{1,0:T(8,128)(2,1)}), bf16[2560,2560]{1,0:T(8,128)(2,1)}) %all-gather.8.cloned.1.call-update) | async-done | bytes 13107216 | tf_op jit(solution)/shard_map/all_gather | solution.py:71
  307.5 9.8 %convolution_add_fusion = f32[256,2560]{1,0:T(8,128)} fusion(bf16[2560,2560]{1,0:T(8,128)(2,1)} %all-gather.8.cloned.1.call-done, f32[2560]{0:T(1024)S(1)} %convert_element_type.64, bf16[256,2560]{1,0:T(8,128)(2,1)S(1)} %copy-done.2, f32[2560]{0:T(1024)S(1)} %convert_element_type.57, f32[256]{0:T(256)S(1)} %add_rsqrt_fusion), kind=kOutput, calls=%fused_computation.17 | convolution fusion | flops 3358720000 | bytes 17060864 | tf_op jit(solution)/shard_map/dot_general | solution.py:76
  317.4 2.1 copy.52
  321.4 1.5 copy-done
  324.0 2.4 copy.62
  326.5 2.3 fusion.15
  328.8 34.0 %all-gather.12.cloned.1.call-done = bf16[2048,512]{0,1:T(8,128)(2,1)} async-done(((bf16[128,512]{0,1:T(8,128)(2,1)}), bf16[2048,512]{0,1:T(8,128)(2,1)}) %all-gather.12.cloned.1.call-update) | async-done | bytes 2097168 | tf_op jit(solution)/shard_map/all_gather | solution.py:107
  362.8 55.9 %all-gather.14.cloned.1.call-done = bf16[2048,512]{0,1:T(8,128)(2,1)} async-done(((bf16[128,512]{0,1:T(8,128)(2,1)}), bf16[2048,512]{0,1:T(8,128)(2,1)}) %all-gather.14.cloned.1.call-update) | async-done | bytes 2097168 | tf_op jit(solution)/shard_map/all_gather | solution.py:108
  418.7 92.3 %while.17 = (s32[]{:T(128)}, f32[4,5,256]{2,1,0:T(8,128)S(1)}, f32[4,5,256]{2,1,0:T(8,128)S(1)}, f32[4,5,256,128]{3,2,1,0:T(8,128)S(1)}, s32[20,2,4]{0,2,1:T(4,1...) while((s32[]{:T(128)}, f32[4,5,256]{2,1,0:T(8,128)S(1)}, ...), condition=%wide.region_7.8_spmd, body=%wide.region_3.7_spmd.sunk | while | flops 343419168 | bytes 15574043 | solution.py:139
  420.0 1.9 fusion.51
  422.6 1.8 multiply_add_fusion.8
  424.4 1.0 constant_dynamic-slice_fusion.3
  425.8 1.9 fusion.51
  428.4 1.8 multiply_add_fusion.8
  430.2 1.0 constant_dynamic-slice_fusion.3
  431.6 1.9 fusion.51
  434.2 1.8 multiply_add_fusion.8
  436.0 1.0 constant_dynamic-slice_fusion.3
  437.4 1.9 fusion.51
  439.9 1.8 multiply_add_fusion.8
  441.7 1.0 constant_dynamic-slice_fusion.3
  443.1 1.9 fusion.51
  445.7 1.8 multiply_add_fusion.8
  447.5 1.0 constant_dynamic-slice_fusion.3
  448.9 1.9 fusion.51
  451.5 1.8 multiply_add_fusion.8
  453.3 1.0 constant_dynamic-slice_fusion.3
  454.7 1.9 fusion.51
  457.2 1.8 multiply_add_fusion.8
  459.1 1.0 constant_dynamic-slice_fusion.3
  460.4 1.9 fusion.51
  463.0 1.8 multiply_add_fusion.8
  464.8 1.0 constant_dynamic-slice_fusion.3
  466.2 1.9 fusion.51
  468.8 1.8 multiply_add_fusion.8
  470.6 1.0 constant_dynamic-slice_fusion.3
  472.0 1.9 fusion.51
  474.6 1.8 multiply_add_fusion.8
  476.4 1.0 constant_dynamic-slice_fusion.3
  477.7 1.9 fusion.51
  480.3 1.8 multiply_add_fusion.8
  482.1 1.0 constant_dynamic-slice_fusion.3
  483.5 1.9 fusion.51
  486.1 1.8 multiply_add_fusion.8
  487.9 1.0 constant_dynamic-slice_fusion.3
  489.3 1.9 fusion.51
  491.9 1.8 multiply_add_fusion.8
  495.1 1.9 fusion.51
  497.6 1.8 multiply_add_fusion.8
  499.5 1.0 constant_dynamic-slice_fusion.3
  500.8 1.9 fusion.51
  503.4 1.8 multiply_add_fusion.8
  505.2 1.0 constant_dynamic-slice_fusion.3
  506.6 1.9 fusion.51
  509.2 1.8 multiply_add_fusion.8
  511.0 2.1 copy.63
  513.1 2.0 broadcast_divide_fusion
  515.1 2.1 copy.64
  (219 shorter events, 27.1 us)
Async XLA Ops:
  7.2 7.5 %copy-start.8 = (f32[64]{0:T(128)S(1)}, f32[64]{0:T(128)}, u32[]{:S(2)}) copy-start(f32[64]{0:T(128)} %constant.155) | copy-start | bytes 772
  7.2 7.5 %copy-start.9 = (f32[64]{0:T(128)S(1)}, f32[64]{0:T(128)}, u32[]{:S(2)}) copy-start(f32[64]{0:T(128)} %constant.157) | copy-start | bytes 772
  7.2 7.5 %copy-start.10 = (f32[64]{0:T(128)S(1)}, f32[64]{0:T(128)}, u32[]{:S(2)}) copy-start(f32[64]{0:T(128)} %constant.159) | copy-start | bytes 772
  7.2 7.5 %copy-start.11 = (f32[64]{0:T(128)S(1)}, f32[64]{0:T(128)}, u32[]{:S(2)}) copy-start(f32[64]{0:T(128)} %constant.161) | copy-start | bytes 772
  7.2 7.1 %copy-start.2 = (bf16[256,2560]{1,0:T(8,128)(2,1)S(1)}, bf16[256,2560]{1,0:T(8,128)(2,1)}, u32[]{:S(2)}) copy-start(bf16[256,2560]{1,0:T(8,128)(2,1)} %param.16) | copy-start | bytes 3932164
  7.2 7.5 %copy-start.5 = (bf16[2560]{0:T(1024)(128)(2,1)S(1)}, bf16[2560]{0:T(1024)(128)(2,1)}, u32[]{:S(2)}) copy-start(bf16[2560]{0:T(1024)(128)(2,1)} %param.21) | copy-start | bytes 15364
  7.2 8.1 %copy-start.6 = (bf16[512]{0:T(512)(128)(2,1)S(1)}, bf16[512]{0:T(512)(128)(2,1)}, u32[]{:S(2)}) copy-start(bf16[512]{0:T(512)(128)(2,1)} %param.22) | copy-start | bytes 3076
  7.2 8.1 %copy-start.7 = (bf16[512]{0:T(512)(128)(2,1)S(1)}, bf16[512]{0:T(512)(128)(2,1)}, u32[]{:S(2)}) copy-start(bf16[512]{0:T(512)(128)(2,1)} %param.23) | copy-start | bytes 3076
  7.3 70.2 %all-gather.6.cloned.1.call-start = ((), (), s32[]{:S(2)}) async-start(), calls=%async_computation | async-start | bytes 2785280 | tf_op jit(solution)/shard_map/all_gather | solution.py:72
  8.0 142.2 %all-gather.10.cloned.1.call-start = ((), (), s32[]{:S(2)}) async-start(), calls=%async_computation.2 | async-start | bytes 2785280 | tf_op jit(solution)/shard_map/all_gather | solution.py:73
  8.7 298.8 %all-gather.8.cloned.1.call-start = ((), (), s32[]{:S(2)}) async-start(), calls=%async_computation.1 | async-start | bytes 13926400 | tf_op jit(solution)/shard_map/all_gather | solution.py:71
  9.5 353.3 %all-gather.12.cloned.1.call-start = ((), (), s32[]{:S(2)}) async-start(), calls=%async_computation.3 | async-start | bytes 2228224 | tf_op jit(solution)/shard_map/all_gather | solution.py:107
  11.2 407.5 %all-gather.14.cloned.1.call-start = ((), (), s32[]{:S(2)}) async-start(), calls=%async_computation.4 | async-start | bytes 2228224 | tf_op jit(solution)/shard_map/all_gather | solution.py:108
  152.8 154.7 %copy-start.3 = (f32[256,512]{1,0:T(8,128)}, f32[256,512]{1,0:T(8,128)S(1)}, u32[]{:S(2)}) copy-start(f32[256,512]{1,0:T(8,128)S(1)} %convolution_add_fusion.1) | copy-start | bytes 1572868
  320.0 1.4 copy-start.1
  321.4 1.5 copy-start
  324.0 94.6 %copy-start.4 = (s32[20,2,4]{0,2,1:T(4,128)S(1)}, s32[20,2,4]{0,2,1:T(4,128)}, u32[]{:S(2)}) copy-start(s32[20,2,4]{0,2,1:T(4,128)} %param.26) | copy-start | bytes 1924
Sparse Core Ops, SparseCore 0:
  9.9 67.5 all-gather.5
  79.3 70.8 all-gather.9
  152.0 155.5 all-gather.7
  309.9 52.7 all-gather.11
  365.1 53.4 all-gather.13
where the time goes:
time: 525 us; the launch traced here: 524 us
  waiting for transfers between devices  377 us (72%)
  matrix products  75.4 us (14%)
  local copies, waits for them, and re-layouts  37.5 us (7%)
  other arithmetic  17.8 us (3%)
  between operations  14.8 us (3%)
    all_gather x1, waiting for transfers between devices, on_device(): lax.all_gather(w_query, 'grp', axis=0, tiled=True)  154 us
    all_gather x1, waiting for transfers between devices, on_device(): lax.all_gather(w_value, 'grp', axis=0, tiled=True)  68.9 us
    all_gather x1, waiting for transfers between devices, on_device(): lax.all_gather(w_key, 'grp', axis=0, tiled=True)  62.1 us
    all_gather x1, waiting for transfers between devices, on_device(): piece_values = lax.all_gather(cache_values, 'ctx', axis=0, tiled=True)  55.9 us
    all_gather x1, waiting for transfers between devices, on_device(): piece_keys = lax.all_gather(cache_keys, 'ctx', axis=0, tiled=True)  34 us
    dot_general x16, matrix products, one_key_block(): jnp.einsum('rkgd,pkd->kgrp', query_heads, block_keys) * score_scale  30.5 us
    dot_general x16, matrix products, one_key_block(): jnp.einsum('kgrp,pkd->kgrd', weights, block_values)  28.4 us
    dynamic_slice x16, local copies, waits for them, and re-layouts, one_key_block(): lax.dynamic_slice_in_dim(piece_values, block_step * QBLK, QBLK, 0)  15.9 us
  transfers between devices with their start and end apart: 5, of which 5 were waited for; matrix products, arithmetic and copies ran while one was open for 6% of the time, Pallas kernels for 0%

commit v1 on v0

--- a/solution.py
+++ b/solution.py
@@ -70,7 +70,9 @@
     panels = (
         lax.all_gather(w_query, "grp", axis=0, tiled=True),
         lax.all_gather(w_key, "grp", axis=0, tiled=True),
-        lax.all_gather(w_value, "grp", axis=0, tiled=True),
+        jnp.concatenate(
+            lax.all_to_all(jnp.stack([w_value] * lax.axis_size("grp")), "grp", 0, 0), axis=0
+        ),
     )
     query_lin, key_lin, value_lin = tuple(
         (jnp.dot(normed, panel, preferred_element_type=jnp.float32) for panel in panels)

time: 525 us -> 489 us (0.931)
  waiting for transfers between devices: 377 us -> 323 us
  starting transfers between devices: 0.19 us -> 10.4 us
    all_gather x1 -> x0, waiting for transfers between devices: 68.9 us -> none  [on_device(): lax.all_gather(w_value, 'grp', axis=0, tiled=True)]
    all_gather x1, waiting for transfers between devices: 62.1 us -> 90.5 us  [on_device(): lax.all_gather(w_key, 'grp', axis=0, tiled=True)]
    all_gather x1, waiting for transfers between devices: 55.9 us -> 33.7 us  [on_device(): piece_values = lax.all_gather(cache_values, 'ctx', axis=0, tiled=True)]
    all_gather x1, waiting for transfers between devices: 34 us -> 55.9 us  [on_device(): piece_keys = lax.all_gather(cache_keys, 'ctx', axis=0, tiled=True)]
    all_gather x1, waiting for transfers between devices: 154 us -> 141 us  [on_device(): lax.all_gather(w_query, 'grp', axis=0, tiled=True)]
    all_to_all x0 -> x1, starting transfers between devices: none -> 10.3 us  [on_device(): lax.all_to_all(jnp.stack([w_value] * lax.axis_size('grp')), 'grp', 0, 0)]
  transfers between devices with their start and end apart: 5 -> 5, of which waited for: 5 -> 4; matrix products, arithmetic and copies ran while one was open for 6% -> 8% of each run, Pallas kernels for 0% -> 0%
where the time goes in v1:
time: 489 us; the launch traced here: 488 us
  waiting for transfers between devices  323 us (66%)
  matrix products  77.4 us (16%)
  local copies, waits for them, and re-layouts  41.3 us (8%)
  other arithmetic  19.6 us (4%)
  between operations  14.7 us (3%)
  starting transfers between devices  10.4 us (2%)
    all_gather x1, waiting for transfers between devices, on_device(): lax.all_gather(w_query, 'grp', axis=0, tiled=True)  141 us
    all_gather x1, waiting for transfers between devices, on_device(): lax.all_gather(w_key, 'grp', axis=0, tiled=True)  90.5 us
    all_gather x1, waiting for transfers between devices, on_device(): piece_keys = lax.all_gather(cache_keys, 'ctx', axis=0, tiled=True)  55.9 us
    all_gather x1, waiting for transfers between devices, on_device(): piece_values = lax.all_gather(cache_values, 'ctx', axis=0, tiled=True)  33.7 us
    dot_general x16, matrix products, one_key_block(): jnp.einsum('rkgd,pkd->kgrp', query_heads, block_keys) * score_scale  30.5 us
    dot_general x16, matrix products, one_key_block(): jnp.einsum('kgrp,pkd->kgrd', weights, block_values)  28.4 us
    dot_general x3, matrix products, on_device(): jnp.dot(normed, panel, preferred_element_type=jnp.float32)  17 us
    dynamic_slice x16, local copies, waits for them, and re-layouts, one_key_block(): lax.dynamic_slice_in_dim(piece_values, block_step * QBLK, QBLK, 0)  15.9 us
  transfers between devices with their start and end apart: 5, of which 4 were waited for; matrix products, arithmetic and copies ran while one was open for 8% of the time, Pallas kernels for 0%

profile of v1, /device:TPU:1, one launch (start us, length us, event | category | flops | bytes accessed | tf_op | source)
XLA Modules:
  0.0 487.8 jit_solution(14242825358918190129)
XLA Ops:
  8.7 1.7 copy.60
  10.4 2.7 stack.2
  13.1 10.3 %all-to-all-start = ((bf16[16,160,512]{2,1,0:T(8,128)(2,1)}), bf16[16,160,512]{2,1,0:T(8,128)(2,1)S(1)}, u32[]{:S(2)}, u32[]{:S(2)}) async-start(bf16[16,160,512]{2,1,0:T(8,128)(2,1)} %stack.2), calls=%async_computation | async-start | bytes 5242880 | tf_op jit(solution)/shard_map/all_to_all | solution.py:74
  26.8 1.7 fusion.9
  28.5 90.5 %all-gather.5.cloned.1.call-done = bf16[2560,512]{1,0:T(8,128)(2,1)} async-done(((bf16[160,512]{1,0:T(8,128)(2,1)}), bf16[2560,512]{1,0:T(8,128)(2,1)}) %all-gather.5.cloned.1.call-update) | async-done | bytes 2621456 | tf_op jit(solution)/shard_map/all_gather | solution.py:72
  119.0 3.8 convolution_add_fusion.2
  122.8 1.2 reshape.573
  125.0 3.0 convolution_add_fusion.1
  128.0 1.1 reshape.579
  129.9 141.5 %all-gather.7.cloned.1.call-done = bf16[2560,2560]{1,0:T(8,128)(2,1)} async-done(((bf16[160,2560]{1,0:T(8,128)(2,1)}), bf16[2560,2560]{1,0:T(8,128)(2,1)}) %all-gather.7.cloned.1.call-update) | async-done | bytes 13107216 | tf_op jit(solution)/shard_map/all_gather | solution.py:71
  271.4 10.2 %convolution_add_fusion = f32[256,2560]{1,0:T(8,128)} fusion(bf16[2560,2560]{1,0:T(8,128)(2,1)} %all-gather.7.cloned.1.call-done, f32[2560]{0:T(1024)} %convert_element_type.64, bf16[256,2560]{1,0:T(8,128)(2,1)} %param.16, f32[2560]{0:T(1024)} %copy-done.4, f32[256]{0:T(256)} %copy-done.9), kind=kOutput, calls=%fused_computation.17 | convolution fusion | flops 3358720000 | bytes 17060864 | tf_op jit(solution)/shard_map/dot_general | solution.py:78
  281.6 2.1 copy.52
  285.7 1.5 copy-done
  288.3 2.4 copy.62
  290.7 2.3 fusion.15
  293.0 33.7 %all-gather.11.cloned.1.call-done = bf16[2048,512]{0,1:T(8,128)(2,1)} async-done(((bf16[128,512]{0,1:T(8,128)(2,1)}), bf16[2048,512]{0,1:T(8,128)(2,1)}) %all-gather.11.cloned.1.call-update) | async-done | bytes 2097168 | tf_op jit(solution)/shard_map/all_gather | solution.py:110
  326.8 55.9 %all-gather.9.cloned.1.call-done = bf16[2048,512]{0,1:T(8,128)(2,1)} async-done(((bf16[128,512]{0,1:T(8,128)(2,1)}), bf16[2048,512]{0,1:T(8,128)(2,1)}) %all-gather.9.cloned.1.call-update) | async-done | bytes 2097168 | tf_op jit(solution)/shard_map/all_gather | solution.py:109
  382.7 92.3 %while.17 = (s32[]{:T(128)}, f32[4,5,256]{2,1,0:T(8,128)S(1)}, f32[4,5,256]{2,1,0:T(8,128)S(1)}, f32[4,5,256,128]{3,2,1,0:T(8,128)S(1)}, s32[20,2,4]{0,2,1:T(4,1...) while((s32[]{:T(128)}, f32[4,5,256]{2,1,0:T(8,128)S(1)}, ...), condition=%wide.region_7.8_spmd, body=%wide.region_3.7_spmd.sunk | while | flops 343419168 | bytes 15574043 | solution.py:141
  384.1 1.9 fusion.51
  386.6 1.8 multiply_add_fusion.8
  388.5 1.0 constant_dynamic-slice_fusion.3
  389.8 1.9 fusion.51
  392.4 1.8 multiply_add_fusion.8
  394.2 1.0 constant_dynamic-slice_fusion.3
  395.6 1.9 fusion.51
  398.2 1.8 multiply_add_fusion.8
  400.0 1.0 constant_dynamic-slice_fusion.3
  401.4 1.9 fusion.51
  403.9 1.8 multiply_add_fusion.8
  405.8 1.0 constant_dynamic-slice_fusion.3
  407.1 1.9 fusion.51
  409.7 1.8 multiply_add_fusion.8
  411.5 1.0 constant_dynamic-slice_fusion.3
  412.9 1.9 fusion.51
  415.5 1.8 multiply_add_fusion.8
  417.3 1.0 constant_dynamic-slice_fusion.3
  418.7 1.9 fusion.51
  421.3 1.8 multiply_add_fusion.8
  423.1 1.0 constant_dynamic-slice_fusion.3
  424.5 1.9 fusion.51
  427.0 1.8 multiply_add_fusion.8
  428.9 1.0 constant_dynamic-slice_fusion.3
  430.2 1.9 fusion.51
  432.8 1.8 multiply_add_fusion.8
  434.6 1.0 constant_dynamic-slice_fusion.3
  436.0 1.9 fusion.51
  438.6 1.8 multiply_add_fusion.8
  441.8 1.9 fusion.51
  444.4 1.8 multiply_add_fusion.8
  446.2 1.0 constant_dynamic-slice_fusion.3
  447.5 1.9 fusion.51
  450.1 1.8 multiply_add_fusion.8
  451.9 1.0 constant_dynamic-slice_fusion.3
  453.3 1.9 fusion.51
  455.9 1.8 multiply_add_fusion.8
  459.1 1.9 fusion.51
  461.7 1.8 multiply_add_fusion.8
  464.9 1.9 fusion.51
  467.4 1.8 multiply_add_fusion.8
  470.6 1.9 fusion.51
  473.2 1.8 multiply_add_fusion.8
  475.0 2.1 copy.63
  477.1 2.0 broadcast_divide_fusion
  479.1 2.1 copy.64
  (223 shorter events, 30.0 us)
Async XLA Ops:
  7.2 111.8 %all-gather.5.cloned.1.call-start = ((), (), s32[]{:S(2)}) async-start(), calls=%async_computation.1 | async-start | bytes 2785280 | tf_op jit(solution)/shard_map/all_gather | solution.py:72
  7.9 263.5 %all-gather.7.cloned.1.call-start = ((), (), s32[]{:S(2)}) async-start(), calls=%async_computation.2 | async-start | bytes 13926400 | tf_op jit(solution)/shard_map/all_gather | solution.py:71
  8.6 318.1 %all-gather.11.cloned.1.call-start = ((), (), s32[]{:S(2)}) async-start(), calls=%async_computation.4 | async-start | bytes 2228224 | tf_op jit(solution)/shard_map/all_gather | solution.py:110
  13.0 10.4 %copy-start.2 = (bf16[128,512]{1,0:T(8,128)(2,1)S(1)}, bf16[128,512]{1,0:T(8,128)(2,1)}, u32[]{:S(2)}) copy-start(bf16[128,512]{1,0:T(8,128)(2,1)} %param.24) | copy-start | bytes 393220
  13.0 11.8 %copy-start.5 = (bf16[2560]{0:T(1024)(128)(2,1)S(1)}, bf16[2560]{0:T(1024)(128)(2,1)}, u32[]{:S(2)}) copy-start(bf16[2560]{0:T(1024)(128)(2,1)} %param.17) | copy-start | bytes 15364
  13.0 11.9 %copy-start.6 = (bf16[2560]{0:T(1024)(128)(2,1)S(1)}, bf16[2560]{0:T(1024)(128)(2,1)}, u32[]{:S(2)}) copy-start(bf16[2560]{0:T(1024)(128)(2,1)} %param.21) | copy-start | bytes 15364
  13.1 12.5 %copy-start.10 = (f32[64]{0:T(128)S(1)}, f32[64]{0:T(128)}, u32[]{:S(2)}) copy-start(f32[64]{0:T(128)} %constant.155) | copy-start | bytes 772
  13.1 12.5 %copy-start.11 = (f32[64]{0:T(128)S(1)}, f32[64]{0:T(128)}, u32[]{:S(2)}) copy-start(f32[64]{0:T(128)} %constant.157) | copy-start | bytes 772
  13.1 12.5 %copy-start.12 = (f32[64]{0:T(128)S(1)}, f32[64]{0:T(128)}, u32[]{:S(2)}) copy-start(f32[64]{0:T(128)} %constant.159) | copy-start | bytes 772
  13.1 12.5 %copy-start.13 = (f32[64]{0:T(128)S(1)}, f32[64]{0:T(128)}, u32[]{:S(2)}) copy-start(f32[64]{0:T(128)} %constant.161) | copy-start | bytes 772
  13.1 13.1 %copy-start.7 = (bf16[512]{0:T(512)(128)(2,1)S(1)}, bf16[512]{0:T(512)(128)(2,1)}, u32[]{:S(2)}) copy-start(bf16[512]{0:T(512)(128)(2,1)} %param.22) | copy-start | bytes 3076
  13.1 13.1 %copy-start.8 = (bf16[512]{0:T(512)(128)(2,1)S(1)}, bf16[512]{0:T(512)(128)(2,1)}, u32[]{:S(2)}) copy-start(bf16[512]{0:T(512)(128)(2,1)} %param.23) | copy-start | bytes 3076
  13.1 111.8 %all-to-all-start = ((bf16[16,160,512]{2,1,0:T(8,128)(2,1)}), bf16[16,160,512]{2,1,0:T(8,128)(2,1)S(1)}, u32[]{:S(2)}, u32[]{:S(2)}) async-start(bf16[16,160,512]{2,1,0:T(8,128)(2,1)} %stack.2), calls=%async_computation | async-start | bytes 5242880 | tf_op jit(solution)/shard_map/all_to_all | solution.py:74
  23.4 359.3 %all-gather.9.cloned.1.call-start = ((), (), s32[]{:S(2)}) async-start(), calls=%async_computation.3 | async-start | bytes 2228224 | tf_op jit(solution)/shard_map/all_gather | solution.py:109
  24.9 94.0 %copy-start.4 = (f32[2560]{0:T(1024)}, f32[2560]{0:T(1024)S(1)}, u32[]{:S(2)}) copy-start(f32[2560]{0:T(1024)S(1)} %convert_element_type.57) | copy-start | bytes 30724
  28.5 90.5 %copy-start.9 = (f32[256]{0:T(256)}, f32[256]{0:T(256)S(1)}, u32[]{:S(2)}) copy-start(f32[256]{0:T(256)S(1)} %add_rsqrt_fusion) | copy-start | bytes 3076
  284.2 1.4 copy-start.1
  285.6 1.5 copy-start
  288.2 94.4 %copy-start.3 = (s32[20,2,4]{0,2,1:T(4,128)S(1)}, s32[20,2,4]{0,2,1:T(4,128)}, u32[]{:S(2)}) copy-start(s32[20,2,4]{0,2,1:T(4,128)} %param.26) | copy-start | bytes 1924
Sparse Core Ops, SparseCore 0:
  9.8 109.1 all-gather.4
  120.7 150.6 all-gather.6
  274.0 52.7 all-gather.10
  329.2 53.4 all-gather.8
